TPU v7x, 256 devices: a whole 4x4x8 slice. The times are simulated.
256 devices in a mesh: seq: 32 (over y, z_lo, core), head: 8 (over x, z_hi).
Axes of the slice: x: 4, y: 4, z: 8 (z_hi: 2, z_lo: 4; z = z_hi * 4 + z_lo), core: 2. Of those that a mesh axis runs over, the one named last changes fastest.
Arguments:
- queries: bfloat16 [4096, 8192], P('seq', 'head'), may hold values from -48 to 48
- keyval: bfloat16 [4096, 2048], P('seq', 'head'), may hold values from -48 to 48
- grad_out: bfloat16 [4096, 8192], P('seq', 'head'), may hold values from -6 to 6
- doc_ids: int32 [4096], P('seq'), may hold values from 0 to 3, never falling along the last dimension, each value on 1 to 2048 neighbouring positions
- deltas: bfloat16 [8, 4096, 8192], P('head', 'seq'), may hold values from -6 to 6
- node_weights: bfloat16 [8192, 2048], P('head', 'seq'), may hold values from -0.0625 to 0.0625
- layer_slot: int32 [8], replicated, may hold values from 0 to 7, each once
Outputs:
- grad_query: bfloat16 [4096, 8192], P('seq', 'head')
- grad_keyval: bfloat16 [4096, 2048], P('seq', 'head')
- scores: float32 [8, 16], replicated
Inputs may be any that keep to these rules, and one draw needn't show every extreme that they name: `layer_slot`: each of the 8 layers stands in exactly one slot. `doc_ids`: never falling along the sequence.
All inputs are finite; a program needn't handle non-finite values.
Results may differ from a plain program's by a relative error of at most 0.013.
Values may be sent and summed in bfloat16 or wider, within the bound.
A program may use at most 64 MiB of HBM per device.

v0:
```python
import math
import jax
import jax.numpy as jnp
from jax import lax
from jax.sharding import PartitionSpec as P

H = 64
KVH = 8
HD = 128


def over_blocks(step, carry, pieces):
    total_rows = pieces[0].shape[0]
    block_rows = 512

    def one_turn(turn_index, running):
        offset = turn_index * block_rows
        blocks = tuple((lax.dynamic_slice_in_dim(piece, offset, block_rows, 0) for piece in pieces))
        return step(running, *blocks, offset)

    return lax.fori_loop(0, total_rows // block_rows, one_turn, carry)


def on_device(queries, keyval, grad_out, doc_ids, deltas, node_weights, layer_slot):
    tok_rows = queries.shape[0]
    kv_local = keyval.shape[1] // (2 * HD)
    group_size = H // KVH
    score_scale = 1.0 / math.sqrt(HD)
    seq_total = tok_rows * lax.axis_size("seq")
    query_grid = queries.reshape(tok_rows, kv_local, group_size, HD)
    out_grid = grad_out.reshape(tok_rows, kv_local, group_size, HD)
    row_positions = lax.axis_index("seq") * tok_rows + jnp.arange(tok_rows, dtype=jnp.int32)

    def block_logits(kv_rows, key_ids, key_start):
        width = kv_rows.shape[0]
        kv_grid = kv_rows.reshape(width, kv_local, 2, HD)
        logits = (
            jnp.einsum(
                "tgie,rge->gitr", query_grid, kv_grid[:, :, 0], preferred_element_type=jnp.float32
            )
            * score_scale
        )
        key_positions = key_start + jnp.arange(width, dtype=jnp.int32)
        allowed = (key_ids[None, :] == doc_ids[:, None]) & (
            key_positions[None, :] <= row_positions[:, None]
        )
        return (logits, allowed, kv_grid)

    def forward_step(carry, kv_rows, key_ids, key_start):
        run_max, run_sum, accum = carry
        logits, allowed, kv_grid = block_logits(kv_rows, key_ids, key_start)
        new_max = jnp.maximum(run_max, jnp.max(jnp.where(allowed, logits, -1e30), axis=3))
        weights = jnp.where(allowed, jnp.exp(logits - new_max[..., None]), 0.0)
        factor = jnp.exp(run_max - new_max)
        run_sum = run_sum * factor + jnp.sum(weights, axis=3)
        values = kv_grid[:, :, 1].astype(jnp.float32)
        accum = accum * factor[..., None] + jnp.einsum(
            "gitr,rge->gite", weights, values, precision=lax.Precision.HIGHEST
        )
        return (new_max, run_sum, accum)

    stat_shape = (kv_local, group_size, tok_rows)
    forward_init = (
        jnp.full(stat_shape, -1e30, jnp.float32),
        jnp.zeros(stat_shape, jnp.float32),
        jnp.zeros(stat_shape + (HD,), jnp.float32),
    )
    run_max, run_sum, accum = over_blocks(
        forward_step,
        forward_init,
        (
            lax.all_gather(keyval, "seq", axis=0, tiled=True),
            lax.all_gather(doc_ids, "seq", axis=0, tiled=True),
        ),
    )
    log_total = run_max + jnp.log(run_sum)
    attn_out = accum / run_sum[..., None]
    row_dot = jnp.einsum(
        "tgie,gite->git", out_grid.astype(jnp.float32), attn_out, precision=lax.Precision.HIGHEST
    )

    def backward_step(carry, kv_rows, key_ids, key_start):
        query_accum = carry[0]
        width = kv_rows.shape[0]
        logits, allowed, kv_grid = block_logits(kv_rows, key_ids, key_start)
        probs = jnp.where(allowed, jnp.exp(logits - log_total[..., None]), 0.0)
        grad_probs = jnp.einsum(
            "tgie,rge->gitr", out_grid, kv_grid[:, :, 1], preferred_element_type=jnp.float32
        )
        grad_logits = (probs * (grad_probs - row_dot[..., None])).astype(jnp.bfloat16)
        query_accum = (
            query_accum
            + jnp.einsum(
                "gitr,rge->gite", grad_logits, kv_grid[:, :, 0], preferred_element_type=jnp.float32
            )
            * score_scale
        )
        probs_low = probs.astype(jnp.bfloat16)
        grad_keys = (
            jnp.einsum(
                "gitr,tgie->rge", grad_logits, query_grid, preferred_element_type=jnp.float32
            )
            * score_scale
        )
        grad_values = jnp.einsum(
            "gitr,tgie->rge", probs_low, out_grid, preferred_element_type=jnp.float32
        )
        block_grad = jnp.stack((grad_keys, grad_values), axis=2).reshape(width, kv_local * 2 * HD)
        kv_buffer = lax.dynamic_update_slice(
            carry[1], block_grad, (key_start, jnp.zeros((), jnp.int32))
        )
        return (query_accum, kv_buffer)

    query_zero = jnp.zeros(stat_shape + (HD,), jnp.float32)
    backward_init = (query_zero, jnp.zeros((seq_total, kv_local * 2 * HD), jnp.float32))
    backward_out = over_blocks(
        backward_step,
        backward_init,
        (
            lax.all_gather(keyval, "seq", axis=0, tiled=True),
            lax.all_gather(doc_ids, "seq", axis=0, tiled=True),
        ),
    )
    query_accum = backward_out[0]
    grad_query = (
        jnp.transpose(query_accum, (2, 0, 1, 3))
        .reshape(tok_rows, kv_local * group_size * HD)
        .astype(jnp.bfloat16)
    )
    grad_keyval = lax.psum_scatter(
        backward_out[1].astype(jnp.bfloat16), "seq", scatter_dimension=0, tiled=True
    )
    width_deltas = lax.all_to_all(deltas, "head", split_axis=2, concat_axis=0, tiled=True)
    grad_rows = lax.all_gather(grad_keyval, "head", axis=1, tiled=True)
    layer_count = width_deltas.shape[0]
    node_count = grad_rows.shape[1] // HD
    projected = jnp.einsum(
        "ltd,dc->ltc",
        width_deltas,
        lax.all_gather(node_weights, "seq", axis=1, tiled=True),
        preferred_element_type=jnp.float32,
    )
    grad_cols = grad_rows.astype(jnp.float32)
    per_column = jnp.sum(projected * grad_cols[None], axis=1)
    partial_value = jnp.sum(per_column.reshape(layer_count, node_count, HD), axis=2)
    totals = lax.psum(partial_value / math.sqrt(seq_total), ("seq", "head"))
    placing = (layer_slot[:, None] == jnp.arange(layer_count, dtype=jnp.int32)[None, :]).astype(
        jnp.float32
    )
    scores = jnp.dot(placing.T, totals, precision=lax.Precision.HIGHEST)
    return (grad_query, grad_keyval, scores)


def solution(mesh):
    return jax.shard_map(
        on_device,
        mesh=mesh,
        in_specs=(
            P("seq", "head"),
            P("seq", "head"),
            P("seq", "head"),
            P("seq"),
            P("head", "seq", None),
            P("head", "seq"),
            P(),
        ),
        out_specs=(P("seq", "head"), P("seq", "head"), P()),
        check_vma=False,
    )
```

profile of v0, /device:TPU:1, one launch (start us, length us, event | category | flops | bytes accessed | tf_op | source)
XLA Modules:
  0.0 491.0 jit_solution(3479772316284741002)
XLA Ops:
  7.2 1.6 copy.67
  12.0 1.7 copy.96
  13.7 46.0 %all-gather = s32[32,1,128]{2,1,0:T(1,128)S(1)} all-gather(s32[1,1,128]{2,1,0:T(1,128)S(1)} %bitcast.262), channel_id=1, replica_groups=mesh['seq'=32,'head'=8] {'seq'}, dimensions={0}, use_global_device_ids=true | all-gather | bytes 16896 | tf_op jit(solution)/shard_map/all_gather | solution.py:121
  59.7 18.1 %all-gather.4.cloned.1.call-done = bf16[4096,256]{0,1:T(8,128)(2,1)} async-done(((bf16[128,256]{0,1:T(8,128)(2,1)}), bf16[4096,256]{0,1:T(8,128)(2,1)}) %all-gather.4.cloned.1.call-update) | async-done | bytes 2097168 | tf_op jit(solution)/shard_map/all_gather | solution.py:120
  77.8 55.1 %while.34 = (s32[]{:T(128)}, f32[1,8,128]{2,1,0:T(8,128)S(1)}, f32[1,8,128]{2,1,0:T(8,128)S(1)}, f32[1,8,128,128]{3,2,1,0:T(8,128)}, s32[4096]{0:T(1024)S(1)}, /...) while((s32[]{:T(128)}, f32[1,8,128]{2,1,0:T(8,128)S(1)}, ...), condition=%wide.region_3.4_spmd.clone, body=%wide.region_0.3_spmd.clone.sunk | while | flops 945363584 | bytes 8728263 | solution.py:21
  79.1 1.4 fusion.67
  80.6 2.8 fusion.70
  86.6 3.8 fusion.70
  92.1 1.4 fusion.67
  93.6 3.8 fusion.70
  100.6 3.8 fusion.70
  107.6 3.8 fusion.70
  113.2 1.4 fusion.67
  114.6 3.8 fusion.70
  120.2 1.4 fusion.67
  121.7 3.8 fusion.70
  127.2 1.4 fusion.67
  128.7 3.8 fusion.70
  135.6 1.6 broadcast_in_dim.87.clone
  137.2 39.6 %while.35 = (s32[]{:T(128)}, f32[1,8,128,128]{3,2,1,0:T(8,128)S(1)}, bf16[4096,256]{1,0:T(8,128)(2,1)}, s32[4096]{0:T(1024)S(1)}, s32[128]{0:T(128)S(1)}, /*inde...) while((s32[]{:T(128)}, ...), condition=%wide.region_5.6_spmd.clone, body=%wide.region_4.5_spmd.clone.sunk | while | flops 675611264 | bytes 14438105 | solution.py:21
  178.3 6.9 %copy.73 = bf16[1,128,8192]{1,0,2:T(2,128)(2,1)} copy(bf16[1,128,8192]{2,1,0:T(8,128)(2,1)S(1)} %copy-done) | data formatting | bytes 4194304 | tf_op args[4]
  185.7 45.2 %reduce.8 = bf16[8192,128]{1,0:T(8,128)(2,1)S(1)} reduce(bf16[8192,1,128]{2,1,0:T(2,128)(2,1)} %bitcast.245, bf16[]{:T(256)} %broadcast.122), dimensions={1}, to_apply=%bitcast.163.reduce_sub_computation | reduce | bytes 4194306
  230.9 3.2 reshape.216
  234.1 54.8 %all_to_all.18 = bf16[8,2,65536]{2,1,0:T(2,128)(2,1)S(1)} all-to-all(bf16[8,2,65536]{2,1,0:T(2,128)(2,1)} %reshape.216), channel_id=1, replica_groups=mesh['seq'=32,'head'=8] {'head'}, dimensions={0} | all-to-all | bytes 4194304 | tf_op jit(solution)/shard_map/all_to_all | solution.py:133
  288.9 4.4 reshape.217
  293.3 2.5 copy.93
  295.8 2.6 copy.74
  299.4 31.5 %reduce-scatter.2.cloned.1.call-done = bf16[128,256]{1,0:T(8,128)(2,1)} async-done(((bf16[4096,256]{1,0:T(8,128)(2,1)}), bf16[128,256]{1,0:T(8,128)(2,1)}) %reduce-scatter.2.cloned.1.call-update) | async-done | bytes 65552 | tf_op jit(solution)/shard_map/reduce_scatter | solution.py:130
  330.9 42.4 %all_gather.17 = bf16[128,2048]{1,0:T(8,128)(2,1)S(1)} all-gather(bf16[128,256]{1,0:T(8,128)(2,1)} %reduce-scatter.2.cloned.1.call-done), channel_id=1, replica_groups=mesh['seq'=32,'head'=8] {'head'}, dimensions={1}, use_global_device_ids=true | all-gather | bytes 589824 | tf_op jit(solution)/shard_map/all_gather | solution.py:134
  374.4 26.8 %all-gather.6.cloned.1.call-done = bf16[1024,2048]{0,1:T(8,128)(2,1)} async-done(((bf16[1024,64]{0,1:T(8,128)(2,1)}), bf16[1024,2048]{0,1:T(8,128)(2,1)}) %all-gather.6.cloned.1.call-update) | async-done | bytes 4194320 | tf_op jit(solution)/shard_map/all_gather | solution.py:140
  401.1 7.2 %multiply_reduce_fusion = f32[8,2048]{1,0:T(8,128)S(1)} fusion(bf16[1024,2048]{0,1:T(8,128)(2,1)} %all-gather.6.cloned.1.call-done, f32[128,2048]{1,0:T(8,128)} %convert_element_type.38, bf16[1,128,8,1024]{3,1,2,0:T(8,128)(2,1)S(1)} %copy-done.1), kind=kOutput, calls=%fused_computation.60 | convolution fusion | flops 4299145216 | bytes 7405568 | tf_op jit(solution)/shard_map/ltd,dc->ltc/dot_general | solution.py:137
  408.4 75.2 %psum.7 = f32[8,16]{0,1:T(8,128)S(1)} all-reduce(f32[8,16]{0,1:T(8,128)S(1)} %broadcast_multiply_fusion), channel_id=1, replica_groups=mesh['seq'=32,'head'=8] {'seq','head'}, use_global_device_ids=true, to_apply=%region_9.10 | all-reduce | flops 128 | bytes 1024 | tf_op jit(solution)/shard_map/psum | solution.py:146
  (212 shorter events, 67.9 us)
Async XLA Ops:
  7.2 6.6 %copy-start.2 = (s32[128]{0:T(128)S(1)}, s32[128]{0:T(128)}, u32[]{:S(2)}) copy-start(s32[128]{0:T(128)} %param.14) | copy-start | bytes 1540
  7.2 70.7 %all-gather.4.cloned.1.call-start = ((), (), s32[]{:S(2)}) async-start(), calls=%async_computation.2 | async-start | bytes 2162688 | tf_op jit(solution)/shard_map/all_gather | solution.py:120
  8.8 322.0 %reduce-scatter.2.cloned.1.call-start = ((), (), s32[]{:S(2)}) async-start(), calls=%async_computation.3 | async-start | bytes 2162688 | tf_op jit(solution)/shard_map/reduce_scatter | solution.py:130
  176.8 1.6 copy-start
  176.8 224.4 %all-gather.6.cloned.1.call-start = ((), (), s32[]{:S(2)}) async-start(), calls=%async_computation.4 | async-start | bytes 4325376 | tf_op jit(solution)/shard_map/all_gather | solution.py:140
  298.4 102.7 %copy-start.1 = (bf16[1,128,8,1024]{3,1,2,0:T(8,128)(2,1)S(1)}, bf16[1,128,8,1024]{3,1,2,0:T(8,128)(2,1)}, u32[]{:S(2)}) copy-start(bf16[1,128,8,1024]{3,1,2,0:T(8,128)(2,1)} %copy.74) | copy-start | bytes 6291460
  374.4 109.2 %copy-start.3 = (s32[8]{0:T(128)S(1)}, s32[8]{0:T(128)}, u32[]{:S(2)}) copy-start(s32[8]{0:T(128)} %param.17) | copy-start | bytes 100
Sparse Core Ops, SparseCore 0:
  10.3 67.4 all-gather.3
  176.9 153.8 reduce-scatter.1
  332.7 68.3 all-gather.5
where the time goes:
time: 493 us; the launch traced here: 491 us
  blocking collectives  218 us (44%)
  waiting for transfers between devices  76.9 us (16%)
  matrix products  70.4 us (14%)
  other arithmetic  56.2 us (11%)
  local copies, waits for them, and re-layouts  53.6 us (11%)
  between operations  13.9 us (3%)
    psum x1, blocking collectives, on_device(): totals = lax.psum(partial_value / math.sqrt(seq_total), ('seq', 'head'))  75.2 us
    all_to_all x1, blocking collectives, on_device(): lax.all_to_all(deltas, 'head', split_axis=2, concat_axis=0, tiled=True)  54.8 us
    unnamed x6, other arithmetic  46.5 us
    all_gather x1, blocking collectives, on_device(): lax.all_gather(doc_ids, 'seq', axis=0, tiled=True)  46 us
    all_gather x1, blocking collectives, on_device(): grad_rows = lax.all_gather(grad_keyval, 'head', axis=1, tiled=True)  42.4 us
    reduce_scatter x1, waiting for transfers between devices, on_device(): lax.psum_scatter(backward_out[1].astype(jnp.bfloat16), 'seq', scatter_dim...  31.5 us
    dot_general x8, matrix products, forward_step(): jnp.einsum('gitr,rge->gite', weights, values, precision=lax.Precision.HIG...  29.4 us
    all_gather x1, waiting for transfers between devices, on_device(): lax.all_gather(node_weights, 'seq', axis=1, tiled=True)  26.8 us
  transfers between devices with their start and end apart: 3, of which 3 were waited for; matrix products, arithmetic and copies ran while one was open for 15% of the time, Pallas kernels for 0%

commit v1 on v0

--- a/solution.py
+++ b/solution.py
@@ -143,7 +143,7 @@
     grad_cols = grad_rows.astype(jnp.float32)
     per_column = jnp.sum(projected * grad_cols[None], axis=1)
     partial_value = jnp.sum(per_column.reshape(layer_count, node_count, HD), axis=2)
-    totals = lax.psum(partial_value / math.sqrt(seq_total), ("seq", "head"))
+    totals = lax.psum(lax.psum(partial_value / math.sqrt(seq_total), "seq"), "head")
     placing = (layer_slot[:, None] == jnp.arange(layer_count, dtype=jnp.int32)[None, :]).astype(
         jnp.float32
     )

time: 493 us -> 515 us (1.045)
  blocking collectives: 218 us -> 237 us
    psum x1 -> x2, blocking collectives: 75.2 us -> 93.6 us  [the longest x1 68 us: on_device(): lax.psum(partial_value / math.sqrt(seq_total), 'seq')]
  transfers between devices with their start and end apart: 3 -> 3, of which waited for: 3 -> 3; matrix products, arithmetic and copies ran while one was open for 15% -> 14% of each run, Pallas kernels for 0% -> 0%
where the time goes in v1:
time: 515 us; the launch traced here: 509 us
  blocking collectives  237 us (46%)
  waiting for transfers between devices  76.9 us (15%)
  matrix products  70.4 us (14%)
  other arithmetic  56.2 us (11%)
  local copies, waits for them, and re-layouts  53.6 us (10%)
  between operations  13.9 us (3%)
    psum x1, blocking collectives, on_device(): lax.psum(partial_value / math.sqrt(seq_total), 'seq')  68 us
    all_to_all x1, blocking collectives, on_device(): lax.all_to_all(deltas, 'head', split_axis=2, concat_axis=0, tiled=True)  54.8 us
    unnamed x6, other arithmetic  46.5 us
    all_gather x1, blocking collectives, on_device(): lax.all_gather(doc_ids, 'seq', axis=0, tiled=True)  46 us
    all_gather x1, blocking collectives, on_device(): grad_rows = lax.all_gather(grad_keyval, 'head', axis=1, tiled=True)  42.4 us
    reduce_scatter x1, waiting for transfers between devices, on_device(): lax.psum_scatter(backward_out[1].astype(jnp.bfloat16), 'seq', scatter_dim...  31.5 us
    dot_general x8, matrix products, forward_step(): jnp.einsum('gitr,rge->gite', weights, values, precision=lax.Precision.HIG...  29.4 us
    all_gather x1, waiting for transfers between devices, on_device(): lax.all_gather(node_weights, 'seq', axis=1, tiled=True)  26.8 us
  transfers between devices with their start and end apart: 3, of which 3 were waited for; matrix products, arithmetic and copies ran while one was open for 14% of the time, Pallas kernels for 0%

profile of v1, /device:TPU:1, one launch (start us, length us, event | category | flops | bytes accessed | tf_op | source)
XLA Modules:
  0.0 509.4 jit_solution(10893737290270238318)
XLA Ops:
  7.2 1.6 copy.67
  12.0 1.7 copy.96
  13.7 46.0 %all-gather = s32[32,1,128]{2,1,0:T(1,128)S(1)} all-gather(s32[1,1,128]{2,1,0:T(1,128)S(1)} %bitcast.262), channel_id=1, replica_groups=mesh['seq'=32,'head'=8] {'seq'}, dimensions={0}, use_global_device_ids=true | all-gather | bytes 16896 | tf_op jit(solution)/shard_map/all_gather | solution.py:121
  59.7 18.1 %all-gather.4.cloned.1.call-done = bf16[4096,256]{0,1:T(8,128)(2,1)} async-done(((bf16[128,256]{0,1:T(8,128)(2,1)}), bf16[4096,256]{0,1:T(8,128)(2,1)}) %all-gather.4.cloned.1.call-update) | async-done | bytes 2097168 | tf_op jit(solution)/shard_map/all_gather | solution.py:120
  77.8 55.1 %while.34 = (s32[]{:T(128)}, f32[1,8,128]{2,1,0:T(8,128)S(1)}, f32[1,8,128]{2,1,0:T(8,128)S(1)}, f32[1,8,128,128]{3,2,1,0:T(8,128)}, s32[4096]{0:T(1024)S(1)}, /...) while((s32[]{:T(128)}, f32[1,8,128]{2,1,0:T(8,128)S(1)}, ...), condition=%wide.region_3.4_spmd.clone, body=%wide.region_0.3_spmd.clone.sunk | while | flops 945363584 | bytes 8728263 | solution.py:21
  79.1 1.4 fusion.67
  80.6 2.8 fusion.70
  86.6 3.8 fusion.70
  92.1 1.4 fusion.67
  93.6 3.8 fusion.70
  100.6 3.8 fusion.70
  107.6 3.8 fusion.70
  114.6 3.8 fusion.70
  120.2 1.4 fusion.67
  121.7 3.8 fusion.70
  127.2 1.4 fusion.67
  128.7 3.8 fusion.70
  135.6 1.6 broadcast_in_dim.87.clone
  137.2 39.6 %while.35 = (s32[]{:T(128)}, f32[1,8,128,128]{3,2,1,0:T(8,128)S(1)}, bf16[4096,256]{1,0:T(8,128)(2,1)}, s32[4096]{0:T(1024)S(1)}, s32[128]{0:T(128)S(1)}, /*inde...) while((s32[]{:T(128)}, ...), condition=%wide.region_5.6_spmd.clone, body=%wide.region_4.5_spmd.clone.sunk | while | flops 675611264 | bytes 14438105 | solution.py:21
  178.3 6.9 %copy.73 = bf16[1,128,8192]{1,0,2:T(2,128)(2,1)} copy(bf16[1,128,8192]{2,1,0:T(8,128)(2,1)S(1)} %copy-done) | data formatting | bytes 4194304 | tf_op args[4]
  185.7 45.2 %reduce.8 = bf16[8192,128]{1,0:T(8,128)(2,1)S(1)} reduce(bf16[8192,1,128]{2,1,0:T(2,128)(2,1)} %bitcast.245, bf16[]{:T(256)} %broadcast.122), dimensions={1}, to_apply=%bitcast.163.reduce_sub_computation | reduce | bytes 4194306
  230.9 3.2 reshape.216
  234.1 54.8 %all_to_all.18 = bf16[8,2,65536]{2,1,0:T(2,128)(2,1)S(1)} all-to-all(bf16[8,2,65536]{2,1,0:T(2,128)(2,1)} %reshape.216), channel_id=1, replica_groups=mesh['seq'=32,'head'=8] {'head'}, dimensions={0} | all-to-all | bytes 4194304 | tf_op jit(solution)/shard_map/all_to_all | solution.py:133
  288.9 4.4 reshape.217
  293.3 2.5 copy.93
  295.8 2.6 copy.74
  299.4 31.5 %reduce-scatter.2.cloned.1.call-done = bf16[128,256]{1,0:T(8,128)(2,1)} async-done(((bf16[4096,256]{1,0:T(8,128)(2,1)}), bf16[128,256]{1,0:T(8,128)(2,1)}) %reduce-scatter.2.cloned.1.call-update) | async-done | bytes 65552 | tf_op jit(solution)/shard_map/reduce_scatter | solution.py:130
  330.9 42.4 %all_gather.17 = bf16[128,2048]{1,0:T(8,128)(2,1)S(1)} all-gather(bf16[128,256]{1,0:T(8,128)(2,1)} %reduce-scatter.2.cloned.1.call-done), channel_id=1, replica_groups=mesh['seq'=32,'head'=8] {'head'}, dimensions={1}, use_global_device_ids=true | all-gather | bytes 589824 | tf_op jit(solution)/shard_map/all_gather | solution.py:134
  374.4 26.8 %all-gather.6.cloned.1.call-done = bf16[1024,2048]{0,1:T(8,128)(2,1)} async-done(((bf16[1024,64]{0,1:T(8,128)(2,1)}), bf16[1024,2048]{0,1:T(8,128)(2,1)}) %all-gather.6.cloned.1.call-update) | async-done | bytes 4194320 | tf_op jit(solution)/shard_map/all_gather | solution.py:140
  401.1 7.2 %multiply_reduce_fusion = f32[8,2048]{1,0:T(8,128)S(1)} fusion(bf16[1024,2048]{0,1:T(8,128)(2,1)} %all-gather.6.cloned.1.call-done, f32[128,2048]{1,0:T(8,128)} %convert_element_type.38, bf16[1,128,8,1024]{3,1,2,0:T(8,128)(2,1)S(1)} %copy-done.1), kind=kOutput, calls=%fused_computation.60 | convolution fusion | flops 4299145216 | bytes 7405568 | tf_op jit(solution)/shard_map/ltd,dc->ltc/dot_general | solution.py:137
  408.4 68.0 %psum.14 = f32[8,16]{0,1:T(8,128)S(1)} all-reduce(f32[8,16]{0,1:T(8,128)S(1)} %broadcast_multiply_fusion), channel_id=1, replica_groups=mesh['seq'=32,'head'=8] {'seq'}, use_global_device_ids=true, to_apply=%region_9.10 | all-reduce | flops 128 | bytes 1024 | tf_op jit(solution)/shard_map/psum | solution.py:146
  476.4 25.6 %psum.15 = f32[8,16]{0,1:T(8,128)S(1)} all-reduce(f32[8,16]{0,1:T(8,128)S(1)} %psum.14), channel_id=1, replica_groups=mesh['seq'=32,'head'=8] {'head'}, use_global_device_ids=true, to_apply=%region_10.11 | all-reduce | flops 128 | bytes 1024 | tf_op jit(solution)/shard_map/psum | solution.py:146
  (213 shorter events, 69.3 us)
Async XLA Ops:
  7.2 6.6 %copy-start.2 = (s32[128]{0:T(128)S(1)}, s32[128]{0:T(128)}, u32[]{:S(2)}) copy-start(s32[128]{0:T(128)} %param.14) | copy-start | bytes 1540
  7.2 70.7 %all-gather.4.cloned.1.call-start = ((), (), s32[]{:S(2)}) async-start(), calls=%async_computation.2 | async-start | bytes 2162688 | tf_op jit(solution)/shard_map/all_gather | solution.py:120
  8.8 322.0 %reduce-scatter.2.cloned.1.call-start = ((), (), s32[]{:S(2)}) async-start(), calls=%async_computation.3 | async-start | bytes 2162688 | tf_op jit(solution)/shard_map/reduce_scatter | solution.py:130
  176.8 1.6 copy-start
  176.8 224.4 %all-gather.6.cloned.1.call-start = ((), (), s32[]{:S(2)}) async-start(), calls=%async_computation.4 | async-start | bytes 4325376 | tf_op jit(solution)/shard_map/all_gather | solution.py:140
  298.4 102.7 %copy-start.1 = (bf16[1,128,8,1024]{3,1,2,0:T(8,128)(2,1)S(1)}, bf16[1,128,8,1024]{3,1,2,0:T(8,128)(2,1)}, u32[]{:S(2)}) copy-start(bf16[1,128,8,1024]{3,1,2,0:T(8,128)(2,1)} %copy.74) | copy-start | bytes 6291460
  374.4 127.7 %copy-start.3 = (s32[8]{0:T(128)S(1)}, s32[8]{0:T(128)}, u32[]{:S(2)}) copy-start(s32[8]{0:T(128)} %param.17) | copy-start | bytes 100
Sparse Core Ops, SparseCore 0:
  10.3 67.4 all-gather.3
  176.9 153.8 reduce-scatter.1
  332.7 68.3 all-gather.5
